TPU v7x, 32 devices: a whole 2x2x4 slice. The times are simulated.
32 devices in a mesh: replica: 4 (over x, core), fsdp: 8 (over z, y).
Axes of the slice: x: 2, y: 2, z: 4, core: 2. Of those that a mesh axis runs over, the one named last changes fastest.
Arguments:
- byte_input: bfloat16 [32768, 768], P(('replica', 'fsdp')), may hold values from -6 to 6
- global_out: bfloat16 [32768, 768], P(('replica', 'fsdp')), may hold values from -6 to 6
- cotangent: bfloat16 [32768, 768], P(('replica', 'fsdp')), may hold values from -6 to 6
- seq_patches: int32 [4, 4], P('replica'), may hold values from 1 to 512, 1024 in all within a row
- last_fill: int32 [4, 4], P('replica'), may hold values from 1 to 8
- deal_slots: int32 [4, 1024], P('replica', 'fsdp'), may hold values from 0 to 1023, as said below
- first_gain: bfloat16 [768], P('fsdp'), may hold values from 0.5 to 1.5
- first_shift: bfloat16 [768], P('fsdp'), may hold values from -1.796875 to 1.796875
- qkv_weight: bfloat16 [768, 2304], P('fsdp'), may hold values from -0.21875 to 0.21875
- out_weight: bfloat16 [768, 768], P('fsdp'), may hold values from -0.4375 to 0.4375
- second_gain: bfloat16 [768], P('fsdp'), may hold values from 0.5 to 1.5
- second_shift: bfloat16 [768], P('fsdp'), may hold values from -1.796875 to 1.796875
- up_weight: bfloat16 [768, 3072], P('fsdp'), may hold values from -0.21875 to 0.21875
- up_bias: bfloat16 [3072], P('fsdp'), may hold values from -3 to 3
- down_weight: bfloat16 [3072, 768], P('fsdp'), may hold values from -0.15625 to 0.15625
- down_bias: bfloat16 [768], P('fsdp'), may hold values from -1.796875 to 1.796875
Outputs:
- layer_out: bfloat16 [32768, 768], P(('replica', 'fsdp'))
- grad_input: bfloat16 [32768, 768], P(('replica', 'fsdp'))
- grad_global: bfloat16 [32768, 768], P(('replica', 'fsdp'))
- grad_first_gain: float32 [768], P('fsdp')
- grad_first_shift: float32 [768], P('fsdp')
- grad_qkv_weight: float32 [768, 2304], P('fsdp')
- grad_out_weight: float32 [768, 768], P('fsdp')
- grad_second_gain: float32 [768], P('fsdp')
- grad_second_shift: float32 [768], P('fsdp')
- grad_up_weight: float32 [768, 3072], P('fsdp')
- grad_up_bias: float32 [3072], P('fsdp')
- grad_down_weight: float32 [3072, 768], P('fsdp')
- grad_down_bias: float32 [768], P('fsdp')
Inputs may be any that keep to these rules, and one draw needn't show every extreme that they name: `seq_patches`: row g gives the patches of the 4 sequences of group g in order; each row sums to 1024 and its largest entry is 512. `last_fill`: bytes used in the last patch of each sequence; the rest of that patch is padding. Each row is a permutation of 0 to 1023. Of the patches p in any aligned block of 128, exactly 16 have deal_slots in each aligned block of 128 positions.
All inputs are finite; a program needn't handle non-finite values.
Results may differ from a plain program's by a relative error of at most 0.017.
Values may be sent and summed in bfloat16 or wider, within the bound.
No kernel may reach another device: no remote copies, remote signals or barrier semaphores. Data moves between devices by JAX's collectives and lax.ppermute only.
A program may use at most 128 MiB of HBM per device.

v0:
```python
import jax
import jax.numpy as jnp
from jax import lax
from jax.sharding import PartitionSpec as P

HEADS = 12
HEAD_DIM = 64
PATCH = 8


EPSILON = 1e-05


def contract_rows(left, right):
    return lax.dot_general(
        left, right, (((0,), (0,)), ((), ())), preferred_element_type=jnp.float32
    )


def contract_cols(left, right):
    return lax.dot_general(
        left, right, (((1,), (1,)), ((), ())), preferred_element_type=jnp.float32
    )


def apply_layer_normalize(values, gain, shift):
    center = values - jnp.mean(values, axis=1, keepdims=True)
    inverse = lax.rsqrt(jnp.mean(jnp.square(center), axis=1, keepdims=True) + EPSILON)
    normed = center * inverse
    return (normed * gain + shift, normed, inverse)


def normalize_pullback(upstream, gain, normed, inverse):
    scaled = upstream * gain
    inner = (
        scaled
        - jnp.mean(scaled, axis=1, keepdims=True)
        - normed * jnp.mean(scaled * normed, axis=1, keepdims=True)
    )
    return (inverse * inner, jnp.sum(upstream * normed, axis=0), jnp.sum(upstream, axis=0))


def block_mask(span):
    index = jnp.arange(span, dtype=jnp.int32)
    return (index[:, None] // PATCH == index[None, :] // PATCH) & (index[None, :] <= index[:, None])


def attention_scores(queries, keys_part, allowed):
    raw = jnp.einsum(
        "gqhd,gkhd->ghqk", queries, keys_part, preferred_element_type=jnp.float32
    ) * HEAD_DIM ** (-0.5)
    return jnp.where(allowed, raw, -1e30)


def body(
    byte_input,
    global_out,
    cotangent,
    seq_patches,
    last_fill,
    deal_slots,
    first_gain,
    first_shift,
    qkv_weight,
    out_weight,
    second_gain,
    second_shift,
    up_weight,
    up_bias,
    down_weight,
    down_bias,
):
    row_count = byte_input.shape[0]
    model_width = byte_input.shape[1]
    patch_count = row_count // PATCH
    fsdp_count = lax.axis_size("fsdp")
    share = patch_count // fsdp_count
    patch_ids = lax.axis_index("fsdp") * patch_count + jnp.arange(patch_count, dtype=jnp.int32)
    seq_ends = jnp.cumsum(seq_patches[0])
    seq_ids = jnp.sum((patch_ids[:, None] >= seq_ends[None, :]).astype(jnp.int32), axis=1)
    seq_hits = (seq_ids[:, None] == jnp.arange(seq_ends.shape[0], dtype=jnp.int32)[None, :]).astype(
        jnp.int32
    )
    end_of = jnp.sum(seq_hits * seq_ends[None, :], axis=1)
    fill_of = jnp.sum(seq_hits * last_fill[0][None, :], axis=1)
    in_patch = jnp.arange(PATCH, dtype=jnp.int32)
    keep_byte = (
        (patch_ids != end_of - 1)[:, None] | (in_patch[None, :] < fill_of[:, None])
    ).reshape(row_count, 1)
    target = deal_slots[0] // patch_count
    dealt_slot = deal_slots[0] % patch_count
    dest_hits = (target[:, None] == jnp.arange(fsdp_count, dtype=jnp.int32)[None, :]).astype(
        jnp.int32
    )
    dest_rank = jnp.sum((jnp.cumsum(dest_hits, axis=0) - 1) * dest_hits, axis=1)
    send_place = target * share + dest_rank
    send_order = (
        jnp.zeros((patch_count,), jnp.int32)
        .at[send_place]
        .set(jnp.arange(patch_count, dtype=jnp.int32))
    )

    def pack_rows(values):
        return values.reshape(patch_count, PATCH, model_width)[send_order].reshape(
            row_count, model_width
        )

    def unpack_rows(values):
        return values.reshape(patch_count, PATCH, model_width)[send_place].reshape(
            row_count, model_width
        )

    arrived, arrived_slot = (
        lax.all_to_all(pack_rows(byte_input), "fsdp", split_axis=0, concat_axis=0, tiled=True),
        lax.all_to_all(dealt_slot[send_order], "fsdp", split_axis=0, concat_axis=0, tiled=True),
    )
    (
        gain_full,
        complete_shift_vector,
        qkv_full,
        outproj_full,
        gain_later,
        deferred_shift_vector,
        expand_full,
        expand_bias,
        reduce_full,
        reduce_bias,
    ) = (
        lax.all_gather(first_gain, "fsdp", axis=0, tiled=True),
        lax.all_gather(first_shift, "fsdp", axis=0, tiled=True),
        lax.all_gather(qkv_weight, "fsdp", axis=0, tiled=True),
        lax.all_gather(out_weight, "fsdp", axis=0, tiled=True),
        lax.all_gather(second_gain, "fsdp", axis=0, tiled=True),
        lax.all_gather(second_shift, "fsdp", axis=0, tiled=True),
        lax.all_gather(up_weight, "fsdp", axis=0, tiled=True),
        lax.all_gather(up_bias, "fsdp", axis=0, tiled=True),
        lax.all_gather(down_weight, "fsdp", axis=0, tiled=True),
        lax.all_gather(down_bias, "fsdp", axis=0, tiled=True),
    )
    attention_norm_gain = gain_full.astype(jnp.float32)
    feedforward_norm_gain = gain_later.astype(jnp.float32)
    global_rows = global_out.reshape(patch_count, PATCH, model_width)[arrived_slot].reshape(
        row_count, model_width
    )
    residual_input = arrived.astype(jnp.float32) + global_rows.astype(jnp.float32)
    attention_normed_input, attention_centered_scaled, attention_inverse_deviation = (
        apply_layer_normalize(
            residual_input, attention_norm_gain, complete_shift_vector.astype(jnp.float32)
        )
    )
    first_in = attention_normed_input.astype(jnp.bfloat16)
    qkv_rows = jnp.dot(first_in, qkv_full, preferred_element_type=jnp.float32).astype(jnp.bfloat16)
    blocks = row_count // 128

    def heads_of(values, start):
        return lax.slice_in_dim(values, start, start + model_width, axis=1).reshape(
            blocks, 128, HEADS, HEAD_DIM
        )

    queries = heads_of(qkv_rows, 0)
    keys_part = heads_of(qkv_rows, model_width)
    values_part = heads_of(qkv_rows, 2 * model_width)
    allowed = block_mask(128)
    scores = attention_scores(queries, keys_part, allowed)
    top_score = jnp.max(scores, axis=3, keepdims=True)
    expo = jnp.exp(scores - top_score)
    total = jnp.sum(expo, axis=3, keepdims=True)
    log_total = top_score + jnp.log(total)
    probs = (expo / total).astype(jnp.bfloat16)
    mixed = jnp.einsum("ghqk,gkhd->gqhd", probs, values_part, preferred_element_type=jnp.float32)
    attended = mixed.reshape(row_count, model_width).astype(jnp.bfloat16)
    residual_midway = residual_input + jnp.dot(
        attended, outproj_full, preferred_element_type=jnp.float32
    )
    feedforward_normed_input, feedforward_centered_scaled, feedforward_inverse_deviation = (
        apply_layer_normalize(
            residual_midway, feedforward_norm_gain, deferred_shift_vector.astype(jnp.float32)
        )
    )
    second_in = feedforward_normed_input.astype(jnp.bfloat16)
    pre_act = jnp.dot(
        second_in, expand_full, preferred_element_type=jnp.float32
    ) + expand_bias.astype(jnp.float32)
    activ = jax.nn.gelu(pre_act, approximate=False).astype(jnp.bfloat16)
    result = (
        residual_midway
        + jnp.dot(activ, reduce_full, preferred_element_type=jnp.float32)
        + reduce_bias.astype(jnp.float32)
    )
    returned = lax.all_to_all(
        result.astype(jnp.bfloat16), "fsdp", split_axis=0, concat_axis=0, tiled=True
    )
    layer_out = jnp.where(keep_byte, unpack_rows(returned), jnp.zeros((), jnp.bfloat16))
    masked_cot = jnp.where(keep_byte, cotangent, jnp.zeros((), jnp.bfloat16))
    upstream_b = lax.all_to_all(
        pack_rows(masked_cot), "fsdp", split_axis=0, concat_axis=0, tiled=True
    )
    upstream = upstream_b.astype(jnp.float32)
    grad_reduce_bias = jnp.sum(upstream, axis=0)
    grad_reduce = contract_rows(activ, upstream_b)
    grad_activ = contract_cols(upstream_b, reduce_full)
    density = jnp.exp(-0.5 * jnp.square(pre_act)) * 0.3989422804014327
    cumulative = 0.5 * (1.0 + jax.scipy.special.erf(pre_act * 0.7071067811865476))
    grad_pre = (grad_activ * (cumulative + pre_act * density)).astype(jnp.bfloat16)
    grad_expand_bias = jnp.sum(grad_pre.astype(jnp.float32), axis=0)
    grad_expand = contract_rows(second_in, grad_pre)
    gradient_feedforward_branch = contract_cols(grad_pre, expand_full)
    normalize_piece, gradient_feedforward_gain, gradient_feedforward_shift = normalize_pullback(
        gradient_feedforward_branch,
        feedforward_norm_gain,
        feedforward_centered_scaled,
        feedforward_inverse_deviation,
    )
    grad_middle = upstream + normalize_piece
    grad_branch = grad_middle.astype(jnp.bfloat16)
    grad_outproj = contract_rows(attended, grad_branch)
    grad_attended = (
        contract_cols(grad_branch, outproj_full)
        .astype(jnp.bfloat16)
        .reshape(blocks, 128, HEADS, HEAD_DIM)
    )
    scores_again = attention_scores(queries, keys_part, allowed)
    probs_again = jnp.exp(scores_again - log_total)
    grad_probs = jnp.einsum(
        "gqhd,gkhd->ghqk", grad_attended, values_part, preferred_element_type=jnp.float32
    )
    grad_values = jnp.einsum(
        "ghqk,gqhd->gkhd",
        probs_again.astype(jnp.bfloat16),
        grad_attended,
        preferred_element_type=jnp.float32,
    )
    grad_scores = (
        probs_again * (grad_probs - jnp.sum(probs_again * grad_probs, axis=3, keepdims=True))
    ).astype(jnp.bfloat16)
    grad_queries = jnp.einsum(
        "ghqk,gkhd->gqhd", grad_scores, keys_part, preferred_element_type=jnp.float32
    ) * HEAD_DIM ** (-0.5)
    grad_keys = jnp.einsum(
        "ghqk,gqhd->gkhd", grad_scores, queries, preferred_element_type=jnp.float32
    ) * HEAD_DIM ** (-0.5)
    grad_qkv = jnp.concatenate(
        [
            grad_queries.reshape(row_count, model_width),
            grad_keys.reshape(row_count, model_width),
            grad_values.reshape(row_count, model_width),
        ],
        axis=1,
    ).astype(jnp.bfloat16)
    grad_qkv_full = contract_rows(first_in, grad_qkv)
    gradient_attention_branch = contract_cols(grad_qkv, qkv_full)
    normalize_before_attention, gradient_attention_gain, gradient_attention_shift = (
        normalize_pullback(
            gradient_attention_branch,
            attention_norm_gain,
            attention_centered_scaled,
            attention_inverse_deviation,
        )
    )
    grad_base = (grad_middle + normalize_before_attention).astype(jnp.bfloat16)
    inverse_slot = (
        jnp.zeros((patch_count,), jnp.int32)
        .at[arrived_slot]
        .set(jnp.arange(patch_count, dtype=jnp.int32))
    )
    grad_global = grad_base.reshape(patch_count, PATCH, model_width)[inverse_slot].reshape(
        row_count, model_width
    )
    sent_back = lax.all_to_all(grad_base, "fsdp", split_axis=0, concat_axis=0, tiled=True)
    grad_input = unpack_rows(sent_back)
    owned = (
        lax.psum_scatter(
            gradient_attention_gain.astype(jnp.bfloat16), "fsdp", scatter_dimension=0, tiled=True
        ).astype(jnp.float32),
        lax.psum_scatter(
            gradient_attention_shift.astype(jnp.bfloat16), "fsdp", scatter_dimension=0, tiled=True
        ).astype(jnp.float32),
        lax.psum_scatter(
            grad_qkv_full.astype(jnp.bfloat16), "fsdp", scatter_dimension=0, tiled=True
        ).astype(jnp.float32),
        lax.psum_scatter(
            grad_outproj.astype(jnp.bfloat16), "fsdp", scatter_dimension=0, tiled=True
        ).astype(jnp.float32),
        lax.psum_scatter(
            gradient_feedforward_gain.astype(jnp.bfloat16), "fsdp", scatter_dimension=0, tiled=True
        ).astype(jnp.float32),
        lax.psum_scatter(
            gradient_feedforward_shift.astype(jnp.bfloat16), "fsdp", scatter_dimension=0, tiled=True
        ).astype(jnp.float32),
        lax.psum_scatter(
            grad_expand.astype(jnp.bfloat16), "fsdp", scatter_dimension=0, tiled=True
        ).astype(jnp.float32),
        lax.psum_scatter(
            grad_expand_bias.astype(jnp.bfloat16), "fsdp", scatter_dimension=0, tiled=True
        ).astype(jnp.float32),
        lax.psum_scatter(
            grad_reduce.astype(jnp.bfloat16), "fsdp", scatter_dimension=0, tiled=True
        ).astype(jnp.float32),
        lax.psum_scatter(
            grad_reduce_bias.astype(jnp.bfloat16), "fsdp", scatter_dimension=0, tiled=True
        ).astype(jnp.float32),
    )
    totals = (
        lax.psum(owned[0].astype(jnp.bfloat16), "replica").astype(jnp.float32),
        lax.psum(owned[1].astype(jnp.bfloat16), "replica").astype(jnp.float32),
        lax.psum(owned[2].astype(jnp.bfloat16), "replica").astype(jnp.float32),
        lax.psum(owned[3].astype(jnp.bfloat16), "replica").astype(jnp.float32),
        lax.psum(owned[4].astype(jnp.bfloat16), "replica").astype(jnp.float32),
        lax.psum(owned[5].astype(jnp.bfloat16), "replica").astype(jnp.float32),
        lax.psum(owned[6].astype(jnp.bfloat16), "replica").astype(jnp.float32),
        lax.psum(owned[7].astype(jnp.bfloat16), "replica").astype(jnp.float32),
        lax.psum(owned[8].astype(jnp.bfloat16), "replica").astype(jnp.float32),
        lax.psum(owned[9].astype(jnp.bfloat16), "replica").astype(jnp.float32),
    )
    return (
        layer_out,
        grad_input,
        grad_global,
        totals[0],
        totals[1],
        totals[2],
        totals[3],
        totals[4],
        totals[5],
        totals[6],
        totals[7],
        totals[8],
        totals[9],
    )


def solution(mesh):
    in_specs = (
        P(("replica", "fsdp"), None),
        P(("replica", "fsdp"), None),
        P(("replica", "fsdp"), None),
        P("replica", None),
        P("replica", None),
        P("replica", "fsdp"),
        P("fsdp"),
        P("fsdp"),
        P("fsdp", None),
        P("fsdp", None),
        P("fsdp"),
        P("fsdp"),
        P("fsdp", None),
        P("fsdp"),
        P("fsdp", None),
        P("fsdp"),
    )
    out_specs = (
        P(("replica", "fsdp"), None),
        P(("replica", "fsdp"), None),
        P(("replica", "fsdp"), None),
        P("fsdp"),
        P("fsdp"),
        P("fsdp", None),
        P("fsdp", None),
        P("fsdp"),
        P("fsdp"),
        P("fsdp", None),
        P("fsdp"),
        P("fsdp", None),
        P("fsdp"),
    )
    return jax.shard_map(body, mesh=mesh, in_specs=in_specs, out_specs=out_specs, check_vma=False)
```

profile of v0, /device:TPU:5, one launch (start us, length us, event | category | flops | bytes accessed | tf_op | source)
XLA Modules:
  0.0 804.0 jit_solution(18170484477021151799)
XLA Ops:
  14.1 5.8 all-to-all-start.1
  31.5 64.7 %all-reduce.12 = (bf16[768]{0:T(1024)(128)(2,1)S(1)}, bf16[768]{0:T(1024)(128)(2,1)S(1)}, bf16[768]{0:T(1024)(128)(2,1)S(1)}, bf16[768]{0:T(1024)(128)(2,1)S(1)}) all-reduce(bf16[768]{0:T(1024)(128)(2,1)S(1)} %dynamic-update-slice.1, bf16[768]{0:T(1024)(128)(2,1)S(1)} %dynamic-update-slice, ...), channel_id=1, replica_groups=mesh['replica'=4,'fsdp'=8] {'fsdp'}, use_global_device_ids=true, to_apply=%add.1 | all-reduce | flops 3072 | bytes 12288
  96.3 22.6 %all-gather = bf16[8,1,384]{2,1,0:T(2,128)(2,1)S(1)} all-gather(bf16[1,1,384]{2,1,0:T(2,128)(2,1)S(1)} %reshape.552), channel_id=1, replica_groups=mesh['replica'=4,'fsdp'=8] {'fsdp'}, dimensions={0}, use_global_device_ids=true | all-gather | bytes 6912 | tf_op jit(solution)/shard_map/all_gather | solution.py:136
  140.2 6.3 convolution_convert_fusion
  174.4 66.6 %all-gather.10.cloned.1.call-done = bf16[768,3072]{1,0:T(8,128)(2,1)} async-done(((bf16[96,3072]{1,0:T(8,128)(2,1)}), bf16[768,3072]{1,0:T(8,128)(2,1)}) %all-gather.10.cloned.1.call-update) | async-done | bytes 4718608 | tf_op jit(solution)/shard_map/all_gather | solution.py:135
  241.0 37.7 %fusion.2 = (bf16[1024,3072]{1,0:T(8,128)(2,1)}, f32[1024,3072]{1,0:T(8,128)}) fusion(f32[3072]{0:T(1024)S(1)} %bitcast.199, bf16[768,3072]{1,0:T(8,128)(2,1)} %all-gather.10.cloned.1.call-done, f32[1024,768]{1,0:T(8,128)} %copy-done.10, f32[768]{0:T(1024)S(1)} %convert_element_type.192, f32[768]{0:T(1024)S(1)} %convert_element_type.191, ...), kind=kOutput, calls=%fused_computation.12 | convolution fusion | flops 5043388416 | bytes 26765312 | tf_op jit(solution)/shard_map/dot_general | solution.py:181
  278.7 42.4 %all-gather.12.cloned.1.call-done = bf16[3072,768]{1,0:T(8,128)(2,1)} async-done(((bf16[384,768]{1,0:T(8,128)(2,1)}), bf16[3072,768]{1,0:T(8,128)(2,1)}) %all-gather.12.cloned.1.call-update) | async-done | bytes 4718608 | tf_op jit(solution)/shard_map/all_gather | solution.py:137
  321.1 12.5 %fusion.61 = (bf16[3072]{0:T(1024)(128)(2,1)S(1)}, bf16[1024,3072]{1,0:T(8,128)(2,1)S(1)}) fusion(f32[1024,3072]{1,0:T(8,128)} %get-tuple-element.60, f32[3072]{0:T(1024)S(1)} %bitcast.200, bf16[1024,768]{1,0:T(8,128)(2,1)} %bitcast.25, bf16[3072,768]{1,0:T(8,128)(2,1)} %all-gather.12.cloned.1.call-done), kind=kOutput, calls=%fused_computation.152 | convolution fusion | flops 4869583872 | bytes 25184256 | tf_op jit(solution)/shard_map/dot_general | solution.py:21
  333.7 5.7 multiply_reduce_fusion.1
  351.4 5.0 multiply_reduce_fusion
  371.1 5.1 fusion.29
  380.8 5.5 convolution_convert_fusion.3
  386.8 10.4 %convolution_convert_fusion.2 = bf16[768,3072]{1,0:T(8,128)(2,1)} fusion(bf16[1024,3072]{1,0:T(8,128)(2,1)} %copy-done.43, f32[1024,768]{1,0:T(8,128)} %copy-done.10, f32[768]{0:T(1024)S(1)} %convert_element_type.192, f32[768]{0:T(1024)S(1)} %convert_element_type.191, f32[1024]{0:T(1024)S(1)} %add_rsqrt_fusion, f32[1024]{0:T(1024)S(1)} %broadcast_multiply_fusion.4), kind=kOutput, calls=%fused_computation.38 | convolution fusion | flops 4838129664 | bytes 14170112 | tf_op jit(solution)/shard_map/dot_general | solution.py:15
  397.2 9.1 %convolution_convert_fusion.1 = bf16[3072,768]{1,0:T(8,128)(2,1)} fusion(bf16[1024,3072]{1,0:T(8,128)(2,1)} %get-tuple-element.59, bf16[1024,768]{1,0:T(8,128)(2,1)} %bitcast.25), kind=kOutput, calls=%fused_computation.37 | convolution fusion | flops 4834197504 | bytes 12582912 | tf_op jit(solution)/shard_map/dot_general | solution.py:15
  409.1 9.6 %multiply_reduce_fusion.2 = (bf16[768]{0:T(1024)(128)(2,1)S(1)}, f32[1024]{0:T(1024)S(1)}, f32[1024]{0:T(1024)S(1)}, bf16[768]{0:T(1024)(128)(2,1)S(1)}, f32[1024,768]{1,0:T(8,128)}) fusion(f32[1024]{0:T(1024)S(1)} %copy-done.26, f32[1024]{0:T(1024)S(1)} %copy-done.22, bf16[128,8,768]{2,1,0:T(8,128)(2,1)S(1)} %copy-done.8, ...), kind=kOutput, calls=%fused_computation.45 | convolution fusion | flops 3633312256 | bytes 14571520 | tf_op jit(solution)/shard_map/dot_general | solution.py:21
  418.8 25.9 %all-reduce.11 = (bf16[768]{0:T(1024)(128)(2,1)S(1)}, bf16[768]{0:T(1024)(128)(2,1)S(1)}, bf16[768]{0:T(1024)(128)(2,1)S(1)}, bf16[768]{0:T(1024)(128)(2,1)S(1)}...) all-reduce(bf16[768]{0:T(1024)(128)(2,1)S(1)} %dynamic-update-slice, ...), channel_id=1, replica_groups=mesh['replica'=4,'fsdp'=8] {'fsdp'}, use_global_device_ids=true, to_apply=%add.4 | all-reduce | flops 7680 | bytes 30720
  444.7 10.0 %add_convert_fusion.1 = bf16[1024,768]{1,0:T(8,128)(2,1)} fusion(f32[1024,768]{1,0:T(8,128)} %copy-done.10, bf16[1024,3072]{1,0:T(8,128)(2,1)} %get-tuple-element.59, bf16[3072,768]{1,0:T(8,128)(2,1)} %all-gather.12.cloned.1.call-done, f32[768]{0:T(1024)S(1)} %convert_element_type.196), kind=kOutput, calls=%fused_computation.53 | convolution fusion | flops 4834197504 | bytes 15731712 | tf_op jit(solution)/shard_map/dot_general | solution.py:187
  454.6 8.6 %all-to-all-start.2 = ((bf16[8,128,768]{2,1,0:T(8,128)(2,1)}), bf16[8,128,768]{2,1,0:T(8,128)(2,1)}, u32[]{:S(2)}, u32[]{:S(2)}) async-start(bf16[8,128,768]{2,1,0:T(8,128)(2,1)} %bitcast.195), calls=%async_computation.2 | async-start | bytes 3145728 | tf_op jit(solution)/shard_map/all_to_all | solution.py:190
  467.7 32.6 %all-to-all-done.2 = bf16[8,128,768]{2,1,0:T(8,128)(2,1)} async-done(((bf16[8,128,768]{2,1,0:T(8,128)(2,1)}), bf16[8,128,768]{2,1,0:T(8,128)(2,1)}, u32[]{:S(2)}, u32[]{:S(2)}) %all-to-all-start.2) | async-done | bytes 1572896 | tf_op jit(solution)/shard_map/all_to_all | solution.py:190
  505.1 36.0 %reduce-scatter.5.cloned.1.call-done = bf16[96,2304]{1,0:T(8,128)(2,1)} async-done(((bf16[768,2304]{1,0:T(8,128)(2,1)}), bf16[96,2304]{1,0:T(8,128)(2,1)}) %reduce-scatter.5.cloned.1.call-update) | async-done | bytes 442384 | tf_op jit(solution)/shard_map/reduce_scatter | solution.py:278
  541.1 101.4 %reduce-scatter.9.cloned.1.call-done = bf16[96,3072]{1,0:T(8,128)(2,1)} async-done(((bf16[768,3072]{1,0:T(8,128)(2,1)}), bf16[96,3072]{1,0:T(8,128)(2,1)}) %reduce-scatter.9.cloned.1.call-update) | async-done | bytes 589840 | tf_op jit(solution)/shard_map/reduce_scatter | solution.py:290
  642.5 98.9 %reduce-scatter.11.cloned.1.call-done = bf16[384,768]{1,0:T(8,128)(2,1)} async-done(((bf16[3072,768]{1,0:T(8,128)(2,1)}), bf16[384,768]{1,0:T(8,128)(2,1)}) %reduce-scatter.11.cloned.1.call-update) | async-done | bytes 589840 | tf_op jit(solution)/shard_map/reduce_scatter | solution.py:296
  744.3 5.7 all-reduce.13
  762.9 27.4 %all-reduce.17.cloned.1.call-done = (bf16[96,2304]{1,0:T(8,128)(2,1)}, bf16[96,768]{1,0:T(8,128)(2,1)}, bf16[96,3072]{1,0:T(8,128)(2,1)}, bf16[384,768]{1,0:T(8,128)(2,1)}) async-done(((bf16[96,2304]{1,0:T(8,128)(2,1)}, bf16[96,768]{1,0:T(8,128)(2,1)}, bf16[96,3072]{1,0:T(8,128)(2,1)}, bf16[384,768]{1,0:T(8,128)(2,1)}), (bf16[96,2304]{1,0:T(8,128)(2,1)}, bf16[96,768]{1,0:T(8,128)(2,1)}, ...) | async-done | bytes 1769488 | tf_op jit(solution)/shard_map/psum | solution.py:306
  (234 shorter events, 131.6 us)
Async XLA Ops:
  7.2 12.7 %copy-start = (bf16[1024,768]{1,0:T(8,128)(2,1)S(1)}, bf16[1024,768]{1,0:T(8,128)(2,1)}, u32[]{:S(2)}) copy-start(bf16[1024,768]{1,0:T(8,128)(2,1)} %param.16) | copy-start | bytes 4718596
  7.2 133.0 %all-gather.6.cloned.1.call-start = ((), (), s32[]{:S(2)}) async-start(), calls=%async_computation.9 | async-start | bytes 3981312 | tf_op jit(solution)/shard_map/all_gather | solution.py:131
  7.9 160.3 %all-gather.8.cloned.1.call-start = ((), (), s32[]{:S(2)}) async-start(), calls=%async_computation.10 | async-start | bytes 1327104 | tf_op jit(solution)/shard_map/all_gather | solution.py:132
  8.7 232.3 %all-gather.10.cloned.1.call-start = ((), (), s32[]{:S(2)}) async-start(), calls=%async_computation.11 | async-start | bytes 5308416 | tf_op jit(solution)/shard_map/all_gather | solution.py:135
  14.1 9.9 %all-to-all-start.1 = ((s32[8,16,1]{1,2,0:T(1,128)}), s32[8,16,1]{1,2,0:T(1,128)S(1)}, u32[]{:S(2)}, u32[]{:S(2)}) async-start(s32[8,16,1]{1,2,0:T(1,128)} %bitcast.11), calls=%async_computation.1 | async-start | bytes 8192 | tf_op jit(solution)/shard_map/all_to_all | solution.py:115
  20.0 76.3 %copy-start.30 = (bf16[384]{0:T(512)(128)(2,1)S(1)}, bf16[384]{0:T(512)(128)(2,1)}, u32[]{:S(2)}) copy-start(bf16[384]{0:T(512)(128)(2,1)} %param.29) | copy-start | bytes 2308
  20.0 99.0 %copy-start.41 = (s32[1,4]{1,0:T(1,128)S(1)}, s32[1,4]{1,0:T(1,128)}, u32[]{:S(2)}) copy-start(s32[1,4]{1,0:T(1,128)} %param.19) | copy-start | bytes 52
  20.0 99.2 %copy-start.31 = (s32[1,4]{1,0:T(1,128)S(1)}, s32[1,4]{1,0:T(1,128)}, u32[]{:S(2)}) copy-start(s32[1,4]{1,0:T(1,128)} %param.20) | copy-start | bytes 52
  24.1 104.5 %all-to-all-start = ((bf16[8,128,768]{2,1,0:T(8,128)(2,1)}), bf16[8,128,768]{2,1,0:T(8,128)(2,1)S(1)}, u32[]{:S(2)}, u32[]{:S(2)}) async-start(bf16[8,128,768]{2,1,0:T(8,128)(2,1)} %bitcast.8), calls=%async_computation | async-start | bytes 3145728 | tf_op jit(solution)/shard_map/all_to_all | solution.py:114
  28.7 292.4 %all-gather.12.cloned.1.call-start = ((), (), s32[]{:S(2)}) async-start(), calls=%async_computation.12 | async-start | bytes 5308416 | tf_op jit(solution)/shard_map/all_gather | solution.py:137
  96.2 40.4 %copy-start.23 = (f32[768]{0:T(1024)}, f32[768]{0:T(1024)S(1)}, u32[]{:S(2)}) copy-start(f32[768]{0:T(1024)S(1)} %convert_element_type.183) | copy-start | bytes 9220
  128.6 150.1 %all-to-all-start.3 = ((bf16[8,128,768]{2,1,0:T(8,128)(2,1)}), bf16[8,128,768]{2,1,0:T(8,128)(2,1)}, u32[]{:S(2)}, u32[]{:S(2)}) async-start(bf16[8,128,768]{2,1,0:T(8,128)(2,1)} %bitcast.186), calls=%async_computation.3 | async-start | bytes 3145728 | tf_op jit(solution)/shard_map/all_to_all | solution.py:195
  133.1 372.0 %reduce-scatter.7.cloned.1.call-start = ((), (), s32[]{:S(2)}) async-start(), calls=%async_computation.14 | async-start | bytes 1327104 | tf_op jit(solution)/shard_map/reduce_scatter | solution.py:281
  321.1 12.6 %copy-start.11 = (f32[1024,768]{1,0:T(8,128)S(1)}, f32[1024,768]{1,0:T(8,128)}, u32[]{:S(2)}) copy-start(f32[1024,768]{1,0:T(8,128)} %copy-done.10) | copy-start | bytes 9437188
  321.1 12.6 %copy-start.35 = (bf16[768,3072]{1,0:T(8,128)(2,1)S(1)}, bf16[768,3072]{1,0:T(8,128)(2,1)}, u32[]{:S(2)}) copy-start(bf16[768,3072]{1,0:T(8,128)(2,1)} %all-gather.10.cloned.1.call-done) | copy-start | bytes 14155780
  363.6 177.5 %reduce-scatter.5.cloned.1.call-start = ((), (), s32[]{:S(2)}) async-start(), calls=%async_computation.13 | async-start | bytes 3981312 | tf_op jit(solution)/shard_map/reduce_scatter | solution.py:278
  386.3 256.2 %reduce-scatter.9.cloned.1.call-start = ((), (), s32[]{:S(2)}) async-start(), calls=%async_computation.15 | async-start | bytes 5308416 | tf_op jit(solution)/shard_map/reduce_scatter | solution.py:290
  397.2 344.2 %reduce-scatter.11.cloned.1.call-start = ((), (), s32[]{:S(2)}) async-start(), calls=%async_computation.16 | async-start | bytes 5308416 | tf_op jit(solution)/shard_map/reduce_scatter | solution.py:296
  454.6 45.7 %all-to-all-start.2 = ((bf16[8,128,768]{2,1,0:T(8,128)(2,1)}), bf16[8,128,768]{2,1,0:T(8,128)(2,1)}, u32[]{:S(2)}, u32[]{:S(2)}) async-start(bf16[8,128,768]{2,1,0:T(8,128)(2,1)} %bitcast.195), calls=%async_computation.2 | async-start | bytes 3145728 | tf_op jit(solution)/shard_map/all_to_all | solution.py:190
  467.7 275.0 %copy-start.33 = (s32[128]{0:T(128)S(1)}, s32[128]{0:T(128)}, u32[]{:S(2)}) copy-start(s32[128]{0:T(128)} %copy-done.32) | copy-start | bytes 1540
  467.7 285.4 %copy-start.9 = (bf16[1024,768]{1,0:T(8,128)(2,1)S(1)}, bf16[1024,768]{1,0:T(8,128)(2,1)}, u32[]{:S(2)}) copy-start(bf16[1024,768]{1,0:T(8,128)(2,1)} %add_convert_fusion) | copy-start | bytes 4718596
  500.3 257.9 %all-to-all-start.4 = ((bf16[8,128,768]{2,1,0:T(8,128)(2,1)}), bf16[8,128,768]{2,1,0:T(8,128)(2,1)S(1)}, u32[]{:S(2)}, u32[]{:S(2)}) async-start(bf16[8,128,768]{2,1,0:T(8,128)(2,1)} %bitcast.174), calls=%async_computation.4 | async-start | bytes 3145728 | tf_op jit(solution)/shard_map/all_to_all | solution.py:269
  505.1 285.2 %all-reduce.17.cloned.1.call-start = ((), (), s32[]{:S(2)}) async-start(), calls=%async_computation.17 | async-start | bytes 3538944 | tf_op jit(solution)/shard_map/psum | solution.py:306
  760.0 37.3 %copy-start.1 = (bf16[1024,768]{1,0:T(8,128)(2,1)S(1)}, bf16[1024,768]{1,0:T(8,128)(2,1)}, u32[]{:S(2)}) copy-start(bf16[1024,768]{1,0:T(8,128)(2,1)} %param.16) | copy-start | bytes 4718596
  (36 other events, 157.4 us)
Sparse Core Ops, SparseCore 0:
  10.2 91.1 all-gather.5
  103.6 41.6 all-gather.7
  147.5 93.4 all-gather.9
  243.0 78.0 all-gather.11
  363.7 61.8 reduce-scatter.6
  429.1 111.9 reduce-scatter.4
  544.8 97.6 reduce-scatter.8
  646.1 95.1 reduce-scatter.10
  744.0 46.2 all-reduce.16
where the time goes:
time: 813 us; the launch traced here: 804 us
  waiting for transfers between devices  410 us (50%)
  matrix products  138 us (17%)
  blocking collectives  119 us (15%)
  local copies, waits for them, and re-layouts  52.5 us (6%)
  other arithmetic  38.7 us (5%)
  starting transfers between devices  29.2 us (4%)
  between operations  16.9 us (2%)
    reduce_scatter x1, waiting for transfers between devices, body(): lax.psum_scatter(grad_expand.astype(jnp.bfloat16), 'fsdp', scatter_dimens...  101 us
    reduce_scatter x1, waiting for transfers between devices, body(): lax.psum_scatter(grad_reduce.astype(jnp.bfloat16), 'fsdp', scatter_dimens...  98.9 us
    unnamed x2, blocking collectives  90.6 us
    all_gather x1, waiting for transfers between devices, body(): lax.all_gather(up_weight, 'fsdp', axis=0, tiled=True)  66.6 us
    all_gather x1, waiting for transfers between devices, body(): lax.all_gather(down_weight, 'fsdp', axis=0, tiled=True)  42.4 us
    dot_general x1, matrix products, body(): jnp.dot(second_in, expand_full, preferred_element_type=jnp.float32)  37.7 us
    reduce_scatter x1, waiting for transfers between devices, body(): lax.psum_scatter(grad_qkv_full.astype(jnp.bfloat16), 'fsdp', scatter_dime...  36 us
    all_to_all x1, waiting for transfers between devices, body(): lax.all_to_all(result.astype(jnp.bfloat16), 'fsdp', split_axis=0, concat_...  32.6 us
  transfers between devices with their start and end apart: 14, of which 8 were waited for; matrix products, arithmetic and copies ran while one was open for 21% of the time, Pallas kernels for 0%

commit v1 on v0

v1 whole, which is shorter than its diff:
```python
import jax
import jax.numpy as jnp
from jax import lax
from jax.sharding import PartitionSpec as P

HEADS = 12
HEAD_DIM = 64
PATCH = 8
EPSILON = 1e-05
BF16 = jnp.bfloat16
F32 = jnp.float32


def contract_rows(left, right):
    return lax.dot_general(left, right, (((0,), (0,)), ((), ())), preferred_element_type=F32)


def contract_cols(left, right):
    return lax.dot_general(left, right, (((1,), (1,)), ((), ())), preferred_element_type=F32)


def apply_layer_normalize(values, gain, shift):
    center = values - jnp.mean(values, axis=1, keepdims=True)
    inverse = lax.rsqrt(jnp.mean(jnp.square(center), axis=1, keepdims=True) + EPSILON)
    normed = center * inverse
    return (normed * gain + shift, normed, inverse)


def normalize_pullback(upstream, gain, normed, inverse):
    scaled = upstream * gain
    inner = (
        scaled
        - jnp.mean(scaled, axis=1, keepdims=True)
        - normed * jnp.mean(scaled * normed, axis=1, keepdims=True)
    )
    return (inverse * inner, jnp.sum(upstream * normed, axis=0), jnp.sum(upstream, axis=0))


def block_mask(span):
    index = jnp.arange(span, dtype=jnp.int32)
    return (index[:, None] // PATCH == index[None, :] // PATCH) & (index[None, :] <= index[:, None])


def attention_scores(queries, keys_part, allowed):
    raw = jnp.einsum(
        "gqhd,gkhd->ghqk", queries, keys_part, preferred_element_type=F32
    ) * HEAD_DIM ** (-0.5)
    return jnp.where(allowed, raw, -1e30)


class Links:
    def __init__(self, n_replica, n_fsdp, shard_rows):
        self.n = {"replica": n_replica, "fsdp": n_fsdp}
        self.at = {"replica": lax.axis_index("replica"), "fsdp": lax.axis_index("fsdp")}
        split = n_replica
        while (shard_rows // split) % 8 or shard_rows % split:
            split //= 2
        self.split = split
        y_count = min(max(n_replica // 2, 1), n_fsdp)

        def bits(low, high):
            found = []
            while low < high:
                found.append(low)
                low *= 2
            return found

        self.core = [("replica", b) for b in bits(1, min(2, split))]
        self.x = [("replica", b) for b in bits(2, split)]
        self.rest = [("replica", b) for b in bits(split, n_replica)]
        self.y = [("fsdp", b) for b in bits(1, y_count)]
        self.z = [("fsdp", b) for b in bits(y_count, n_fsdp)]
        self.quarter = self.at["replica"] % split

    def swap(self, values, step):
        axis, mask = step
        return lax.ppermute(values, axis, [(i, i ^ mask) for i in range(self.n[axis])])

    def my_bit(self, step):
        axis, mask = step
        return (self.at[axis] // mask) % 2

    def gather(self, piece, steps):
        for step in steps:
            piece = jnp.concatenate([piece, self.swap(piece, step)], axis=0)
        return piece

    def place_of(self, steps):
        shards = jnp.arange(self.n["fsdp"], dtype=jnp.int32)[:, None]
        quarters = jnp.arange(self.split, dtype=jnp.int32)[None, :]
        apart = {"fsdp": shards ^ self.at["fsdp"], "replica": quarters ^ self.quarter}
        place = jnp.zeros((self.n["fsdp"], self.split), jnp.int32)
        for position, (axis, mask) in enumerate(steps):
            place = place + ((apart[axis] // mask) % 2) * (1 << position)
        return place.reshape(-1)

    def reduce(self, values, steps):
        axes = list(reversed(self.z)) + list(reversed(self.y)) + list(reversed(self.x)) + self.core
        rest = values.shape[2:]
        values = values.reshape((2,) * len(axes) + rest)
        for step in steps:
            dim = axes.index(step)
            mine = self.my_bit(step)
            keep = lax.dynamic_index_in_dim(values, mine, dim, keepdims=False)
            send = lax.dynamic_index_in_dim(values, 1 - mine, dim, keepdims=False)
            got = self.swap(send, step)
            values = (keep.astype(F32) + got.astype(F32)).astype(BF16)
            axes.remove(step)
        for step in self.rest:
            values = (values.astype(F32) + self.swap(values, step).astype(F32)).astype(BF16)
        return values.reshape(rest)


def body(
    byte_input,
    global_out,
    cotangent,
    seq_patches,
    last_fill,
    deal_slots,
    first_gain,
    first_shift,
    qkv_weight,
    out_weight,
    second_gain,
    second_shift,
    up_weight,
    up_bias,
    down_weight,
    down_bias,
):
    row_count = byte_input.shape[0]
    model_width = byte_input.shape[1]
    patch_count = row_count // PATCH
    fsdp_count = lax.axis_size("fsdp")
    replica_count = lax.axis_size("replica")
    share = patch_count // fsdp_count
    shard = qkv_weight.shape[0]
    links = Links(replica_count, fsdp_count, shard)
    split = links.split
    part = shard // split
    down_part = down_weight.shape[0] // split
    ff = up_weight.shape[1]
    blocks_up = ff // model_width

    target = deal_slots[0] // patch_count
    dealt_slot = deal_slots[0] % patch_count
    dest_hits = (target[:, None] == jnp.arange(fsdp_count, dtype=jnp.int32)[None, :]).astype(jnp.int32)
    dest_rank = jnp.sum((jnp.cumsum(dest_hits, axis=0) - 1) * dest_hits, axis=1)
    send_place = target * share + dest_rank
    send_order = (
        jnp.zeros((patch_count,), jnp.int32)
        .at[send_place]
        .set(jnp.arange(patch_count, dtype=jnp.int32))
    )
    wanted_slot = lax.all_to_all(
        dealt_slot[send_order], "fsdp", split_axis=0, concat_axis=0, tiled=True
    )

    def pick(values, order):
        return values.reshape(patch_count, PATCH, model_width)[order].reshape(row_count, model_width)

    arrived = lax.all_to_all(
        pick(global_out, wanted_slot), "fsdp", split_axis=0, concat_axis=0, tiled=True
    )

    def my_part(values, size):
        return lax.dynamic_slice_in_dim(values, links.quarter * size, size, axis=0)

    def cut(values):
        return [
            lax.slice_in_dim(values, i * model_width, (i + 1) * model_width, axis=1)
            for i in range(values.shape[1] // model_width)
        ]

    small = jnp.concatenate([first_gain, first_shift, second_gain, second_shift, down_bias])
    small = jnp.pad(small, (0, model_width - small.shape[0]))
    bias_row = jnp.pad(up_bias, (0, model_width - up_bias.shape[0]))
    vectors = jnp.pad(jnp.stack([small, bias_row]), ((0, 6), (0, 0)))

    qkv_mine = my_part(qkv_weight, part)
    out_mine = my_part(out_weight, part)
    up_mine = my_part(up_weight, part)
    down_mine = my_part(down_weight, down_part)
    q_mine, k_mine, v_mine = cut(qkv_mine)
    first_piece = jnp.concatenate([vectors, q_mine, k_mine, v_mine, out_mine], axis=0)
    second_piece = jnp.concatenate(cut(up_mine), axis=0)
    third_piece = down_mine

    z_steps = list(reversed(links.z))
    order_a = links.y + links.x + links.core
    order_b = links.x + links.y + links.core
    place_a = links.place_of(z_steps + order_a)
    place_b = links.place_of(z_steps + order_b)

    def gather_group(piece, at):
        rows = piece.shape[0]
        got = links.gather(piece[None], z_steps)
        a = links.gather(got[:, :at], order_a)
        b = links.gather(got[:, at:], order_b)
        a = a[place_a].reshape(fsdp_count, split, at, model_width)
        b = b[place_b].reshape(fsdp_count, split, rows - at, model_width)
        return a, b

    def block_of(values, start):
        return lax.slice_in_dim(values, start, start + part, axis=2).reshape(model_width, model_width)

    g1a, g1b = gather_group(first_piece, 8 + 2 * part)
    vec = g1a[:, 0, :8]
    widths = [0, 1, 2, 3, 4]
    gain_full, shift_full, gain_later, shift_later, reduce_bias = [
        vec[:, 0, i * shard : (i + 1) * shard].reshape(model_width).astype(F32) for i in widths
    ]
    expand_bias = vec[:, 1, : up_bias.shape[0]].reshape(ff).astype(F32)
    qkv_full = jnp.concatenate(
        [block_of(g1a, 8), block_of(g1a, 8 + part), block_of(g1b, 0)], axis=1
    )
    outproj_full = block_of(g1b, part)
    half_up = blocks_up // 2
    g2a, g2b = gather_group(second_piece, half_up * part)
    expand_full = jnp.concatenate(
        [block_of(g2a, i * part) for i in range(half_up)]
        + [block_of(g2b, i * part) for i in range(blocks_up - half_up)],
        axis=1,
    )
    g3a, g3b = gather_group(third_piece, down_part // 2)
    reduce_full = jnp.concatenate([g3a, g3b], axis=2).reshape(ff, model_width)

    patch_ids = lax.axis_index("fsdp") * patch_count + jnp.arange(patch_count, dtype=jnp.int32)
    seq_ends = jnp.cumsum(seq_patches[0])
    seq_ids = jnp.sum((patch_ids[:, None] >= seq_ends[None, :]).astype(jnp.int32), axis=1)
    seq_hits = (seq_ids[:, None] == jnp.arange(seq_ends.shape[0], dtype=jnp.int32)[None, :]).astype(jnp.int32)
    end_of = jnp.sum(seq_hits * seq_ends[None, :], axis=1)
    fill_of = jnp.sum(seq_hits * last_fill[0][None, :], axis=1)
    in_patch = jnp.arange(PATCH, dtype=jnp.int32)
    keep_byte = (
        (patch_ids != end_of - 1)[:, None] | (in_patch[None, :] < fill_of[:, None])
    ).reshape(row_count, 1)

    residual_input = byte_input.astype(F32) + pick(arrived, send_place).astype(F32)
    attention_normed_input, attention_centered_scaled, attention_inverse_deviation = (
        apply_layer_normalize(residual_input, gain_full, shift_full)
    )
    first_in = attention_normed_input.astype(BF16)
    qkv_rows = jnp.dot(first_in, qkv_full, preferred_element_type=F32).astype(BF16)
    blocks = row_count // 128

    def heads_of(values, start):
        return lax.slice_in_dim(values, start, start + model_width, axis=1).reshape(
            blocks, 128, HEADS, HEAD_DIM
        )

    queries = heads_of(qkv_rows, 0)
    keys_part = heads_of(qkv_rows, model_width)
    values_part = heads_of(qkv_rows, 2 * model_width)
    allowed = block_mask(128)
    scores = attention_scores(queries, keys_part, allowed)
    top_score = jnp.max(scores, axis=3, keepdims=True)
    expo = jnp.exp(scores - top_score)
    total = jnp.sum(expo, axis=3, keepdims=True)
    log_total = top_score + jnp.log(total)
    probs = (expo / total).astype(BF16)
    mixed = jnp.einsum("ghqk,gkhd->gqhd", probs, values_part, preferred_element_type=F32)
    attended = mixed.reshape(row_count, model_width).astype(BF16)
    residual_midway = residual_input + jnp.dot(attended, outproj_full, preferred_element_type=F32)
    feedforward_normed_input, feedforward_centered_scaled, feedforward_inverse_deviation = (
        apply_layer_normalize(residual_midway, gain_later, shift_later)
    )
    second_in = feedforward_normed_input.astype(BF16)
    pre_act = jnp.dot(second_in, expand_full, preferred_element_type=F32) + expand_bias
    cumulative = 0.5 * (1.0 + jax.scipy.special.erf(pre_act * 0.7071067811865476))
    activ = (pre_act * cumulative).astype(BF16)
    result = residual_midway + jnp.dot(activ, reduce_full, preferred_element_type=F32) + reduce_bias
    layer_out = jnp.where(keep_byte, result, 0.0).astype(BF16)

    upstream_b = jnp.where(keep_byte, cotangent, jnp.zeros((), BF16))
    upstream = upstream_b.astype(F32)
    grad_reduce_bias = jnp.sum(upstream, axis=0)
    grad_reduce = contract_rows(activ, upstream_b)
    grad_activ = contract_cols(upstream_b, reduce_full)
    density = jnp.exp(-0.5 * jnp.square(pre_act)) * 0.3989422804014327
    grad_pre = (grad_activ * (cumulative + pre_act * density)).astype(BF16)
    grad_expand_bias = jnp.sum(grad_pre.astype(F32), axis=0)
    grad_expand = contract_rows(second_in, grad_pre)
    gradient_feedforward_branch = contract_cols(grad_pre, expand_full)
    normalize_piece, gradient_feedforward_gain, gradient_feedforward_shift = normalize_pullback(
        gradient_feedforward_branch,
        gain_later,
        feedforward_centered_scaled,
        feedforward_inverse_deviation,
    )
    grad_middle = upstream + normalize_piece
    grad_branch = grad_middle.astype(BF16)
    grad_outproj = contract_rows(attended, grad_branch)
    grad_attended = (
        contract_cols(grad_branch, outproj_full)
        .astype(BF16)
        .reshape(blocks, 128, HEADS, HEAD_DIM)
    )
    scores_again = attention_scores(queries, keys_part, allowed)
    probs_again = jnp.exp(scores_again - log_total)
    grad_probs = jnp.einsum(
        "gqhd,gkhd->ghqk", grad_attended, values_part, preferred_element_type=F32
    )
    grad_values = jnp.einsum(
        "ghqk,gqhd->gkhd", probs_again.astype(BF16), grad_attended, preferred_element_type=F32
    )
    grad_scores = (
        probs_again * (grad_probs - jnp.sum(probs_again * grad_probs, axis=3, keepdims=True))
    ).astype(BF16)
    grad_queries = jnp.einsum(
        "ghqk,gkhd->gqhd", grad_scores, keys_part, preferred_element_type=F32
    ) * HEAD_DIM ** (-0.5)
    grad_keys = jnp.einsum(
        "ghqk,gqhd->gkhd", grad_scores, queries, preferred_element_type=F32
    ) * HEAD_DIM ** (-0.5)
    grad_qkv = jnp.concatenate(
        [
            grad_queries.reshape(row_count, model_width),
            grad_keys.reshape(row_count, model_width),
            grad_values.reshape(row_count, model_width),
        ],
        axis=1,
    ).astype(BF16)
    gradient_attention_branch = contract_cols(grad_qkv, qkv_full)
    normalize_before_attention, gradient_attention_gain, gradient_attention_shift = (
        normalize_pullback(
            gradient_attention_branch,
            gain_full,
            attention_centered_scaled,
            attention_inverse_deviation,
        )
    )
    grad_input = (grad_middle + normalize_before_attention).astype(BF16)
    sent_back = lax.all_to_all(
        pick(grad_input, send_order), "fsdp", split_axis=0, concat_axis=0, tiled=True
    )
    inverse_slot = (
        jnp.zeros((patch_count,), jnp.int32)
        .at[wanted_slot]
        .set(jnp.arange(patch_count, dtype=jnp.int32))
    )
    grad_global = pick(sent_back, inverse_slot)
    grad_qkv_full = contract_rows(first_in, grad_qkv)

    red_a = links.core + links.x + links.y + links.z
    red_b = links.core + links.y + links.x + links.z

    def parts_of(values):
        return values.reshape(fsdp_count, split, values.shape[0] // (fsdp_count * split), -1)

    def owned(values, at):
        a = links.reduce(values[:, :, :at].astype(BF16), red_a)
        b = links.reduce(values[:, :, at:].astype(BF16), red_b)
        total = jnp.concatenate([a, b], axis=0)[None]
        steps = links.core + links.x
        total = links.gather(total, steps)
        quarters = jnp.arange(split, dtype=jnp.int32) ^ links.quarter
        place = jnp.zeros((split,), jnp.int32)
        for position, (_, mask) in enumerate(steps):
            place = place + ((quarters // mask) % 2) * (1 << position)
        return total[place].astype(F32)

    def column_blocks(values):
        return jnp.concatenate([parts_of(v) for v in cut(values)], axis=2)

    r3 = owned(parts_of(grad_reduce), down_part // 2)
    r2 = owned(column_blocks(grad_expand), half_up * part)
    vec_rows = jnp.concatenate(
        [
            v.reshape(fsdp_count, shard)
            for v in (
                gradient_attention_gain,
                gradient_attention_shift,
                gradient_feedforward_gain,
                gradient_feedforward_shift,
                grad_reduce_bias,
            )
        ],
        axis=1,
    )
    vec_rows = jnp.pad(vec_rows, ((0, 0), (0, model_width - vec_rows.shape[1])))
    bias_rows = grad_expand_bias.reshape(fsdp_count, -1)
    bias_rows = jnp.pad(bias_rows, ((0, 0), (0, model_width - bias_rows.shape[1])))
    vec_rows = jnp.pad(jnp.stack([vec_rows, bias_rows], axis=1), ((0, 0), (0, 6), (0, 0)))
    vec_rows = jnp.broadcast_to(vec_rows[:, None], (fsdp_count, split, 8, model_width))
    r1 = owned(
        jnp.concatenate([vec_rows, column_blocks(grad_qkv_full), parts_of(grad_outproj)], axis=2),
        8 + 2 * part,
    )

    def rows_of(values, start):
        return values[:, start : start + part].reshape(shard, model_width)

    own_vec = [r1[0, 0, i * shard : (i + 1) * shard] for i in range(5)]
    own_bias = r1[0, 1, : up_bias.shape[0]]
    return (
        layer_out,
        grad_input,
        grad_global,
        own_vec[0],
        own_vec[1],
        jnp.concatenate([rows_of(r1, 8 + i * part) for i in range(3)], axis=1),
        rows_of(r1, 8 + 3 * part),
        own_vec[2],
        own_vec[3],
        jnp.concatenate([rows_of(r2, i * part) for i in range(blocks_up)], axis=1),
        own_bias,
        r3.reshape(down_weight.shape[0], model_width),
        own_vec[4],
    )


def solution(mesh):
    in_specs = (
        P(("replica", "fsdp"), None),
        P(("replica", "fsdp"), None),
        P(("replica", "fsdp"), None),
        P("replica", None),
        P("replica", None),
        P("replica", "fsdp"),
        P("fsdp"),
        P("fsdp"),
        P("fsdp", None),
        P("fsdp", None),
        P("fsdp"),
        P("fsdp"),
        P("fsdp", None),
        P("fsdp"),
        P("fsdp", None),
        P("fsdp"),
    )
    out_specs = (
        P(("replica", "fsdp"), None),
        P(("replica", "fsdp"), None),
        P(("replica", "fsdp"), None),
        P("fsdp"),
        P("fsdp"),
        P("fsdp", None),
        P("fsdp", None),
        P("fsdp"),
        P("fsdp"),
        P("fsdp", None),
        P("fsdp"),
        P("fsdp", None),
        P("fsdp"),
    )
    return jax.shard_map(body, mesh=mesh, in_specs=in_specs, out_specs=out_specs, check_vma=False)
```

time: 813 us -> 515 us (0.63)
  waiting for transfers between devices: 410 us -> 120 us
  blocking collectives: 119 us -> 0 us
  local copies, waits for them, and re-layouts: 52.5 us -> 120 us
  starting transfers between devices: 29.2 us -> 78 us
  other arithmetic: 38.7 us -> 74.1 us
  matrix products: 138 us -> 110 us
  between operations: 16.9 us -> 2.72 us
    reduce_scatter x4 -> x0, waiting for transfers between devices: 236 us -> none  [the longest x1 101 us: body(): lax.psum_scatter(grad_expand.astype(jnp.bfloat16), 'fsdp', scatter_dimens...]
    ppermute x0 -> x60, waiting for transfers between devices: none -> 120 us  [swap(): lax.ppermute(values, axis, [(i, i ^ mask) for i in range(self.n[axis])])]
    all_gather x4 -> x0, waiting for transfers between devices: 109 us -> none  [the longest x1 66.6 us: body(): lax.all_gather(up_weight, 'fsdp', axis=0, tiled=True)]
    unnamed x2 -> x0, blocking collectives: 90.6 us -> none
    ppermute x0 -> x60, starting transfers between devices: none -> 59.8 us  [swap(): lax.ppermute(values, axis, [(i, i ^ mask) for i in range(self.n[axis])])]
    concatenate x0 -> x35, other arithmetic: none -> 40.4 us  [the longest x30 30.5 us: gather(): piece = jnp.concatenate([piece, self.swap(piece, step)], axis=0)]
    all_to_all x4 -> x2, waiting for transfers between devices: 32.6 us -> 0.01 us  [the longest x1 0.01 us: body(): lax.all_to_all(pick(global_out, wanted_slot), 'fsdp', split_axis=0, conca...]
    psum x1 -> x0, waiting for transfers between devices: 27.4 us -> none  [body(): lax.psum(owned[2].astype(jnp.bfloat16), 'replica').astype(jnp.float32)]
  transfers between devices with their start and end apart: 14 -> 63, of which waited for: 8 -> 21; matrix products, arithmetic and copies ran while one was open for 21% -> 22% of each run, Pallas kernels for 0% -> 0%
where the time goes in v1:
time: 515 us; the launch traced here: 505 us
  local copies, waits for them, and re-layouts  120 us (23%)
  waiting for transfers between devices  120 us (23%)
  matrix products  110 us (21%)
  starting transfers between devices  78 us (15%)
  other arithmetic  74.1 us (14%)
    ppermute x60, waiting for transfers between devices, swap(): lax.ppermute(values, axis, [(i, i ^ mask) for i in range(self.n[axis])])  120 us
    ppermute x60, starting transfers between devices, swap(): lax.ppermute(values, axis, [(i, i ^ mask) for i in range(self.n[axis])])  59.8 us
    dot_general x4, matrix products, contract_cols(): lax.dot_general(left, right, (((1,), (1,)), ((), ())), preferred_element_...  34.7 us
    concatenate x30, other arithmetic, gather(): piece = jnp.concatenate([piece, self.swap(piece, step)], axis=0)  30.5 us
    dot_general x4, matrix products, contract_rows(): lax.dot_general(left, right, (((0,), (0,)), ((), ())), preferred_element_...  30.5 us
    unnamed x157, local copies, waits for them, and re-layouts  24.9 us
    dot_general x1, matrix products, body(): jnp.dot(second_in, expand_full, preferred_element_type=F32) + expand_bias  11.6 us
    gather x3, local copies, waits for them, and re-layouts, gather_group(): a = a[place_a].reshape(fsdp_count, split, at, model_width)  11.6 us
  transfers between devices with their start and end apart: 63, of which 21 were waited for; matrix products, arithmetic and copies ran while one was open for 22% of the time, Pallas kernels for 0%

profile of v1, /device:TPU:5, one launch (start us, length us, event | category | flops | bytes accessed | tf_op | source)
XLA Modules:
  0.0 505.2 jit_solution(4232774098281121651)
XLA Ops:
  5.5 5.8 %all-to-all-start = ((s32[8,16,1]{1,2,0:T(1,128)}), s32[8,16,1]{1,2,0:T(1,128)S(1)}, u32[]{:S(2)}, u32[]{:S(2)}) async-start(s32[8,16,1]{1,2,0:T(1,128)} %bitcast.8), calls=%async_computation | async-start | bytes 8192 | tf_op jit(solution)/shard_map/all_to_all | solution.py:156
  36.2 5.4 %collective-permute-done.9 = bf16[2,96,768]{2,1,0:T(8,128)(2,1)S(1)} collective-permute-done((bf16[2,96,768]{2,1,0:T(8,128)(2,1)S(1)}, bf16[2,96,768]{2,1,0:T(8,128)(2,1)S(1)}, u32[]{:S(2)}, u32[]{:S(2)}) %collective-permute-start.9) | collective-permute-done | bytes 294944 | tf_op jit(solution)/shard_map/ppermute | solution.py:77
  41.8 6.1 %collective-permute-done.17 = bf16[2,96,768]{2,1,0:T(8,128)(2,1)S(1)} collective-permute-done((bf16[2,96,768]{2,1,0:T(8,128)(2,1)S(1)}, bf16[2,96,768]{2,1,0:T(8,128)(2,1)S(1)}, u32[]{:S(2)}, u32[]{:S(2)}) %collective-permute-start.17) | collective-permute-done | bytes 294944 | tf_op jit(solution)/shard_map/ppermute | solution.py:77
  50.9 6.0 %all-to-all-start.1 = ((bf16[8,128,768]{2,1,0:T(8,128)(2,1)}), bf16[8,128,768]{2,1,0:T(8,128)(2,1)S(1)}, u32[]{:S(2)}, u32[]{:S(2)}) async-start(bf16[8,128,768]{2,1,0:T(8,128)(2,1)} %bitcast.10), calls=%async_computation.1 | async-start | bytes 3145728 | tf_op jit(solution)/shard_map/all_to_all | solution.py:163
  64.6 5.7 %collective-permute-done.21 = bf16[4,48,768]{2,1,0:T(8,128)(2,1)S(1)} collective-permute-done((bf16[4,48,768]{2,1,0:T(8,128)(2,1)S(1)}, bf16[4,48,768]{2,1,0:T(8,128)(2,1)S(1)}, u32[]{:S(2)}, u32[]{:S(2)}) %collective-permute-start.21) | collective-permute-done | bytes 294944 | tf_op jit(solution)/shard_map/ppermute | solution.py:77
  70.7 6.0 %collective-permute-done.5 = bf16[4,48,768]{2,1,0:T(8,128)(2,1)S(1)} collective-permute-done((bf16[4,48,768]{2,1,0:T(8,128)(2,1)S(1)}, bf16[4,48,768]{2,1,0:T(8,128)(2,1)S(1)}, u32[]{:S(2)}, u32[]{:S(2)}) %collective-permute-start.5) | collective-permute-done | bytes 294944 | tf_op jit(solution)/shard_map/ppermute | solution.py:77
  77.0 12.3 %collective-permute-done.11 = bf16[8,48,768]{2,1,0:T(8,128)(2,1)S(1)} collective-permute-done((bf16[8,48,768]{2,1,0:T(8,128)(2,1)S(1)}, bf16[8,48,768]{2,1,0:T(8,128)(2,1)S(1)}, u32[]{:S(2)}, u32[]{:S(2)}) %collective-permute-start.11) | collective-permute-done | bytes 589856 | tf_op jit(solution)/shard_map/ppermute | solution.py:77
  89.7 12.2 %collective-permute-done.19 = bf16[8,48,768]{2,1,0:T(8,128)(2,1)S(1)} collective-permute-done((bf16[8,48,768]{2,1,0:T(8,128)(2,1)S(1)}, bf16[8,48,768]{2,1,0:T(8,128)(2,1)S(1)}, u32[]{:S(2)}, u32[]{:S(2)}) %collective-permute-start.19) | collective-permute-done | bytes 589856 | tf_op jit(solution)/shard_map/ppermute | solution.py:77
  110.8 8.5 %collective-permute-done.6 = bf16[8,48,768]{2,1,0:T(8,128)(2,1)S(1)} collective-permute-done((bf16[8,48,768]{2,1,0:T(8,128)(2,1)S(1)}, bf16[8,48,768]{2,1,0:T(8,128)(2,1)S(1)}, u32[]{:S(2)}, u32[]{:S(2)}) %collective-permute-start.6) | collective-permute-done | bytes 589856 | tf_op jit(solution)/shard_map/ppermute | solution.py:77
  152.1 5.2 %pad_maximum_fusion.1 = bf16[8,4,96,768]{3,2,1,0:T(8,128)(2,1)} fusion(bf16[8,4,48,768]{3,2,1,0:T(8,128)(2,1)} %bitcast.391, bf16[8,4,48,768]{3,2,1,0:T(8,128)(2,1)} %bitcast.390), kind=kLoop, calls=%fused_computation.33 | loop fusion | flops 9437184 | bytes 9437184 | tf_op jit(solution)/shard_map/concatenate | solution.py:227
  188.2 6.3 %convolution_convert_fusion = bf16[1024,2304]{1,0:T(8,128)(2,1)S(1)} fusion(bf16[768,768]{1,0:T(8,128)(2,1)} %bitcast.432, bf16[768,768]{1,0:T(8,128)(2,1)} %bitcast.436, bf16[768,768]{1,0:T(8,128)(2,1)} %bitcast.434, f32[768]{0:T(1024)S(1)} %reshape.1125, f32[768]{0:T(1024)S(1)} %reshape.1124, bf16[1024,768]{1,0:T(8,128)(2,1)S(1)} %copy-done.3, ...), kind=kOutput, calls=%fused_computation.26 | convolution fusion | flops 3643146240 | bytes 11417600 | tf_op jit(solution)/shard_map/dot_general | solution.py:245
  225.8 11.6 %multiply_convert_fusion.1 = (bf16[1024,3072]{1,0:T(8,128)(2,1)}, f32[1024,3072]{1,0:T(8,128)}) fusion(f32[3072]{0:T(1024)S(1)} %bitcast.450, bf16[768,768]{1,0:T(8,128)(2,1)} %bitcast.446, bf16[768,768]{1,0:T(8,128)(2,1)} %bitcast.444, bf16[768,768]{1,0:T(8,128)(2,1)S(1)} %bitcast.442, bf16[768,768]{1,0:T(8,128)(2,1)S(1)} %bitcast.440, ...), kind=kOutput, calls=%fused_computation.18 | convolution fusion | flops 4873519104 | bytes 26765312 | tf_op jit(solution)/shard_map/dot_general | solution.py:270
  237.5 16.8 %convert_reduce_fusion = (bf16[3072]{0:T(1024)(128)(2,1)S(1)}, bf16[1024,3072]{1,0:T(8,128)(2,1)}) fusion(f32[1024,3072]{1,0:T(8,128)} %get-tuple-element.84, f32[3072]{0:T(1024)S(1)} %bitcast.451, bf16[3072,768]{1,0:T(8,128)(2,1)S(1)} %bitcast.415, bf16[1024,768]{1,0:T(8,128)(2,1)S(1)} %copy-done.48, pred[1024]{0:T(1024)(128)(4,1)} %or.17), kind=kOutput, calls=%fused_computation.16 | convolution fusion | flops 4873516032 | bytes 25185280 | tf_op jit(solution)/shard_map/dot_general | solution.py:19
  254.3 9.1 %multiply_reduce_fusion.1 = (bf16[768]{0:T(1024)(128)(2,1)}, f32[1024]{0:T(1024)S(1)}, f32[1024]{0:T(1024)S(1)}, bf16[768]{0:T(1024)(128)(2,1)}, f32[1024,768]{1,0:T(8,128)S(1)}) fusion(f32[1024,768]{1,0:T(8,128)S(1)} %get-tuple-element.82, f32[1024]{0:T(1024)S(1)} %add_rsqrt_fusion, f32[1024]{0:T(1024)S(1)} %broadcast_multiply_fusion.4, ...), kind=kOutput, calls=%fused_computation.39 | convolution fusion | flops 4857786368 | bytes 17324032 | tf_op jit(solution)/shard_map/dot_general | solution.py:19
  263.4 9.9 %convolution_convert_fusion.2 = bf16[768,3072]{1,0:T(8,128)(2,1)} fusion(bf16[1024,3072]{1,0:T(8,128)(2,1)} %get-tuple-element.90, f32[1024,768]{1,0:T(8,128)S(1)} %get-tuple-element.82, f32[768]{0:T(1024)S(1)} %copy-done.66, f32[768]{0:T(1024)S(1)} %reshape.1126, f32[1024]{0:T(1024)S(1)} %add_rsqrt_fusion, f32[1024]{0:T(1024)S(1)} %broadcast_multiply_fusion.4), kind=kOutput, calls=%fused_computation.29 | convolution fusion | flops 4838129664 | bytes 14170112 | tf_op jit(solution)/shard_map/dot_general | solution.py:15
  281.9 6.4 %fusion.26 = bf16[8,128,12,64]{1,3,2,0:T(8,128)(2,1)} fusion(f32[8,12,128,128]{2,3,1,0:T(8,128)} %copy-done.2, f32[8,12,128]{2,1,0:T(8,128)S(1)} %log_add_fusion, bf16[8,128,12,64]{1,0,3,2:T(8,128)(2,1)S(1)} %bitcast.374), kind=kOutput, calls=%fused_computation.104 | convolution fusion | flops 205258752 | bytes 9486336 | tf_op jit(solution)/shard_map/ghqk,gqhd->gkhd/dot_general | solution.py:305
  304.2 6.2 %multiply_reduce_fusion.2 = (bf16[768]{0:T(1024)(128)(2,1)S(1)}, f32[1024]{0:T(1024)S(1)}, f32[1024]{0:T(1024)S(1)}, bf16[768]{0:T(1024)(128)(2,1)S(1)}, f32[1024,768]{1,0:T(8,128)}) fusion(f32[1024]{0:T(1024)S(1)} %add_rsqrt_fusion.1, f32[1024]{0:T(1024)S(1)} %broadcast_multiply_fusion.5, bf16[128,8,768]{2,1,0:T(8,128)(2,1)S(1)} %gather_fusion.2, ...), kind=kOutput, calls=%fused_computation.40 | convolution fusion | flops 3643929088 | bytes 14571520 | tf_op jit(solution)/shard_map/dot_general | solution.py:19
  310.4 6.3 %convolution_convert_fusion.3 = bf16[768,2304]{1,0:T(8,128)(2,1)} fusion(bf16[1024,2304]{0,1:T(8,128)(2,1)S(1)} %bitcast_dynamic-update-slice_fusion, f32[768]{0:T(1024)S(1)} %copy-done.64, f32[768]{0:T(1024)S(1)} %reshape.1124, bf16[1024,768]{1,0:T(8,128)(2,1)S(1)} %copy-done.4, bf16[128,8,768]{2,1,0:T(8,128)(2,1)S(1)} %gather_fusion.2, ...), kind=kOutput, calls=%fused_computation.30 | convolution fusion | flops 3631939584 | bytes 11417600 | tf_op jit(solution)/shard_map/dot_general | solution.py:15
  316.8 9.5 %convolution_convert_fusion.1 = bf16[3072,768]{1,0:T(8,128)(2,1)} fusion(bf16[1024,3072]{1,0:T(8,128)(2,1)} %get-tuple-element.83, bf16[1024,768]{1,0:T(8,128)(2,1)} %param.18, pred[1024]{0:T(1024)(128)(4,1)S(1)} %copy-done.62), kind=kOutput, calls=%fused_computation.28 | convolution fusion | flops 4834983936 | bytes 12583936 | tf_op jit(solution)/shard_map/dot_general | solution.py:15
  326.3 9.6 %select_convert_fusion = bf16[1024,768]{1,0:T(8,128)(2,1)} fusion(f32[1024,768]{1,0:T(8,128)S(1)} %copy-done.6, bf16[1024,3072]{1,0:T(8,128)(2,1)} %get-tuple-element.83, bf16[3072,768]{1,0:T(8,128)(2,1)} %bitcast.412, f32[768]{0:T(1024)S(1)} %reshape.1129, pred[1024]{0:T(1024)(128)(4,1)S(1)} %copy-done.62), kind=kOutput, calls=%fused_computation.47 | convolution fusion | flops 4834983936 | bytes 15732736 | tf_op jit(solution)/shard_map/dot_general | solution.py:273
  371.6 6.5 %all-to-all-start.2 = ((bf16[8,128,768]{2,1,0:T(8,128)(2,1)}), bf16[8,128,768]{2,1,0:T(8,128)(2,1)S(1)}, u32[]{:S(2)}, u32[]{:S(2)}) async-start(bf16[8,128,768]{2,1,0:T(8,128)(2,1)} %bitcast.40), calls=%async_computation.2 | async-start | bytes 3145728 | tf_op jit(solution)/shard_map/all_to_all | solution.py:335
  393.6 14.2 %collective-permute-done.54 = bf16[2,2,2,48,768]{4,3,2,1,0:T(8,128)(2,1)S(1)} collective-permute-done((bf16[2,2,2,48,768]{4,3,2,1,0:T(8,128)(2,1)S(1)}, bf16[2,2,2,48,768]{4,3,2,1,0:T(8,128)(2,1)S(1)}, u32[]{:S(2)}, u32[]{:S(2)}) %collective-permute-start.54) | collective-permute-done | bytes 589856 | tf_op jit(solution)/shard_map/ppermute | solution.py:77
  409.8 11.0 %collective-permute-done.42 = bf16[2,2,2,48,768]{4,3,2,1,0:T(8,128)(2,1)S(1)} collective-permute-done((bf16[2,2,2,48,768]{4,3,2,1,0:T(8,128)(2,1)S(1)}, bf16[2,2,2,48,768]{4,3,2,1,0:T(8,128)(2,1)S(1)}, u32[]{:S(2)}, u32[]{:S(2)}) %collective-permute-start.42) | collective-permute-done | bytes 589856 | tf_op jit(solution)/shard_map/ppermute | solution.py:77
  424.1 9.3 %collective-permute-done.30 = bf16[2,2,2,48,768]{4,3,2,1,0:T(8,128)(2,1)S(1)} collective-permute-done((bf16[2,2,2,48,768]{4,3,2,1,0:T(8,128)(2,1)S(1)}, bf16[2,2,2,48,768]{4,3,2,1,0:T(8,128)(2,1)S(1)}, u32[]{:S(2)}, u32[]{:S(2)}) %collective-permute-start.30) | collective-permute-done | bytes 589856 | tf_op jit(solution)/shard_map/ppermute | solution.py:77
  (506 shorter events, 296.7 us)
Async XLA Ops:
  50.9 120.4 %all-to-all-start.1 = ((bf16[8,128,768]{2,1,0:T(8,128)(2,1)}), bf16[8,128,768]{2,1,0:T(8,128)(2,1)S(1)}, u32[]{:S(2)}, u32[]{:S(2)}) async-start(bf16[8,128,768]{2,1,0:T(8,128)(2,1)} %bitcast.10), calls=%async_computation.1 | async-start | bytes 3145728 | tf_op jit(solution)/shard_map/all_to_all | solution.py:163
  60.7 28.6 %collective-permute-start.11 = (bf16[8,48,768]{2,1,0:T(8,128)(2,1)S(1)}, bf16[8,48,768]{2,1,0:T(8,128)(2,1)S(1)}, u32[]{:S(2)}, u32[]{:S(2)}) collective-permute-start(bf16[8,48,768]{2,1,0:T(8,128)(2,1)S(1)} %pad_maximum_fusion.27), channel_id=1, source_target_pairs={{0,16},{8,24},{16,0},{24,8},{1,17},{9,25},{17,1},{25,9},{2,18},{10... | collective-permute-start | bytes 1769480 | tf_op jit(solution)/shard_map/ppermute | solution.py:77
  62.1 39.9 %collective-permute-start.19 = (bf16[8,48,768]{2,1,0:T(8,128)(2,1)S(1)}, bf16[8,48,768]{2,1,0:T(8,128)(2,1)S(1)}, u32[]{:S(2)}, u32[]{:S(2)}) collective-permute-start(bf16[8,48,768]{2,1,0:T(8,128)(2,1)S(1)} %pad_maximum_fusion.30), channel_id=1, source_target_pairs={{0,16},{8,24},{16,0},{24,8},{1,17},{9,25},{17,1},{25,9},{2,18},{10... | collective-permute-start | bytes 1769480 | tf_op jit(solution)/shard_map/ppermute | solution.py:77
  64.5 41.9 %collective-permute-start.2 = (bf16[4,56,768]{2,1,0:T(8,128)(2,1)S(1)}, bf16[4,56,768]{2,1,0:T(8,128)(2,1)S(1)}, u32[]{:S(2)}, u32[]{:S(2)}) collective-permute-start(bf16[4,56,768]{2,1,0:T(8,128)(2,1)S(1)} %slice.261), channel_id=1, source_target_pairs={{0,1},{1,0},{2,3},{3,2},{4,5},{5,4},{6,7},{7,6},{8,9},{9,8},{10,11... | collective-permute-start | bytes 1032200 | tf_op jit(solution)/shard_map/ppermute | solution.py:77
  70.3 36.3 %collective-permute-start.14 = (bf16[8,48,768]{2,1,0:T(8,128)(2,1)S(1)}, bf16[8,48,768]{2,1,0:T(8,128)(2,1)S(1)}, u32[]{:S(2)}, u32[]{:S(2)}) collective-permute-start(bf16[8,48,768]{2,1,0:T(8,128)(2,1)S(1)} %pad_maximum_fusion.28), channel_id=1, source_target_pairs={{0,1},{1,0},{2,3},{3,2},{4,5},{5,4},{6,7},{7,6},{8,9},{9,8},{10,11... | collective-permute-start | bytes 1769480 | tf_op jit(solution)/shard_map/ppermute | solution.py:77
  76.6 32.5 %collective-permute-start.22 = (bf16[8,48,768]{2,1,0:T(8,128)(2,1)S(1)}, bf16[8,48,768]{2,1,0:T(8,128)(2,1)S(1)}, u32[]{:S(2)}, u32[]{:S(2)}) collective-permute-start(bf16[8,48,768]{2,1,0:T(8,128)(2,1)S(1)} %pad_maximum_fusion.31), channel_id=1, source_target_pairs={{0,1},{1,0},{2,3},{3,2},{4,5},{5,4},{6,7},{7,6},{8,9},{9,8},{10,11... | collective-permute-start | bytes 1769480 | tf_op jit(solution)/shard_map/ppermute | solution.py:77
  89.3 30.1 %collective-permute-start.6 = (bf16[8,48,768]{2,1,0:T(8,128)(2,1)S(1)}, bf16[8,48,768]{2,1,0:T(8,128)(2,1)S(1)}, u32[]{:S(2)}, u32[]{:S(2)}) collective-permute-start(bf16[8,48,768]{2,1,0:T(8,128)(2,1)S(1)} %pad_maximum_fusion.25), channel_id=1, source_target_pairs={{0,1},{1,0},{2,3},{3,2},{4,5},{5,4},{6,7},{7,6},{8,9},{9,8},{10,11... | collective-permute-start | bytes 1769480 | tf_op jit(solution)/shard_map/ppermute | solution.py:77
  106.4 24.9 %collective-permute-start.20 = (bf16[16,48,768]{2,1,0:T(8,128)(2,1)}, bf16[16,48,768]{2,1,0:T(8,128)(2,1)}, u32[]{:S(2)}, u32[]{:S(2)}) collective-permute-start(bf16[16,48,768]{2,1,0:T(8,128)(2,1)} %pad_maximum_fusion.16), channel_id=1, source_target_pairs={{0,8},{8,0},{16,24},{24,16},{1,9},{9,1},{17,25},{25,17},{2,10},{10... | collective-permute-start | bytes 3538952 | tf_op jit(solution)/shard_map/ppermute | solution.py:77
  109.1 29.2 %collective-permute-start.15 = (bf16[16,48,768]{2,1,0:T(8,128)(2,1)}, bf16[16,48,768]{2,1,0:T(8,128)(2,1)}, u32[]{:S(2)}, u32[]{:S(2)}) collective-permute-start(bf16[16,48,768]{2,1,0:T(8,128)(2,1)} %pad_maximum_fusion.15), channel_id=1, source_target_pairs={{0,8},{8,0},{16,24},{24,16},{1,9},{9,1},{17,25},{25,17},{2,10},{10... | collective-permute-start | bytes 3538952 | tf_op jit(solution)/shard_map/ppermute | solution.py:77
  119.4 25.9 %collective-permute-start.23 = (bf16[16,48,768]{2,1,0:T(8,128)(2,1)}, bf16[16,48,768]{2,1,0:T(8,128)(2,1)}, u32[]{:S(2)}, u32[]{:S(2)}) collective-permute-start(bf16[16,48,768]{2,1,0:T(8,128)(2,1)} %pad_maximum_fusion.17), channel_id=1, source_target_pairs={{0,8},{8,0},{16,24},{24,16},{1,9},{9,1},{17,25},{25,17},{2,10},{10... | collective-permute-start | bytes 3538952 | tf_op jit(solution)/shard_map/ppermute | solution.py:77
  123.5 37.9 %collective-permute-start.7 = (bf16[16,48,768]{2,1,0:T(8,128)(2,1)}, bf16[16,48,768]{2,1,0:T(8,128)(2,1)}, u32[]{:S(2)}, u32[]{:S(2)}) collective-permute-start(bf16[16,48,768]{2,1,0:T(8,128)(2,1)} %pad_maximum_fusion.13), channel_id=1, source_target_pairs={{0,8},{8,0},{16,24},{24,16},{1,9},{9,1},{17,25},{25,17},{2,10},{10... | collective-permute-start | bytes 3538952 | tf_op jit(solution)/shard_map/ppermute | solution.py:77
  125.8 49.9 %collective-permute-start.4 = (bf16[16,56,768]{2,1,0:T(8,128)(2,1)}, bf16[16,56,768]{2,1,0:T(8,128)(2,1)}, u32[]{:S(2)}, u32[]{:S(2)}) collective-permute-start(bf16[16,56,768]{2,1,0:T(8,128)(2,1)} %pad_maximum_fusion.12), channel_id=1, source_target_pairs={{0,8},{8,0},{16,24},{24,16},{1,9},{9,1},{17,25},{25,17},{2,10},{10... | collective-permute-start | bytes 4128776 | tf_op jit(solution)/shard_map/ppermute | solution.py:77
  355.1 24.6 %collective-permute-start.53 = (bf16[2,2,2,2,48,768]{5,4,3,2,1,0:T(8,128)(2,1)}, bf16[2,2,2,2,48,768]{5,4,3,2,1,0:T(8,128)(2,1)}, u32[]{:S(2)}, u32[]{:S(2)}) collective-permute-start(bf16[2,2,2,2,48,768]{5,4,3,2,1,0:T(8,128)(2,1)} %dynamic-slice_bitcast_fusion.1), channel_id=1, source_target_pairs={{0,8},{8,0},{16,24},{24,16},{1,9},{9,1},{17,25},{25,17},{2,10},{10... | collective-permute-start | bytes 3538952 | tf_op jit(solution)/shard_map/ppermute | solution.py:77
  355.6 27.4 %collective-permute-start.48 = (bf16[2,2,2,2,48,768]{5,4,0,1,2,3:T(8,128)(2,1)}, bf16[2,2,2,2,48,768]{5,4,0,1,2,3:T(8,128)(2,1)}, u32[]{:S(2)}, u32[]{:S(2)}) collective-permute-start(bf16[2,2,2,2,48,768]{5,4,0,1,2,3:T(8,128)(2,1)} %bitcast.368), channel_id=1, source_target_pairs={{0,8},{8,0},{16,24},{24,16},{1,9},{9,1},{17,25},{25,17},{2,10},{10... | collective-permute-start | bytes 3538952 | tf_op jit(solution)/shard_map/ppermute | solution.py:77
  356.8 28.0 %collective-permute-start.41 = (bf16[2,2,2,2,48,768]{5,4,3,2,1,0:T(8,128)(2,1)}, bf16[2,2,2,2,48,768]{5,4,3,2,1,0:T(8,128)(2,1)}, u32[]{:S(2)}, u32[]{:S(2)}) collective-permute-start(bf16[2,2,2,2,48,768]{5,4,3,2,1,0:T(8,128)(2,1)} %fusion.41), channel_id=1, source_target_pairs={{0,8},{8,0},{16,24},{24,16},{1,9},{9,1},{17,25},{25,17},{2,10},{10... | collective-permute-start | bytes 3538952 | tf_op jit(solution)/shard_map/ppermute | solution.py:77
  357.3 30.3 %collective-permute-start.36 = (bf16[2,2,2,2,48,768]{5,4,0,1,2,3:T(8,128)(2,1)}, bf16[2,2,2,2,48,768]{5,4,0,1,2,3:T(8,128)(2,1)}, u32[]{:S(2)}, u32[]{:S(2)}) collective-permute-start(bf16[2,2,2,2,48,768]{5,4,0,1,2,3:T(8,128)(2,1)} %bitcast.367), channel_id=1, source_target_pairs={{0,8},{8,0},{16,24},{24,16},{1,9},{9,1},{17,25},{25,17},{2,10},{10... | collective-permute-start | bytes 3538952 | tf_op jit(solution)/shard_map/ppermute | solution.py:77
  364.1 26.7 %collective-permute-start.29 = (bf16[2,2,2,2,48,768]{5,4,3,2,1,0:T(8,128)(2,1)}, bf16[2,2,2,2,48,768]{5,4,3,2,1,0:T(8,128)(2,1)}, u32[]{:S(2)}, u32[]{:S(2)}) collective-permute-start(bf16[2,2,2,2,48,768]{5,4,3,2,1,0:T(8,128)(2,1)} %fusion.47), channel_id=1, source_target_pairs={{0,8},{8,0},{16,24},{24,16},{1,9},{9,1},{17,25},{25,17},{2,10},{10... | collective-permute-start | bytes 3538952 | tf_op jit(solution)/shard_map/ppermute | solution.py:77
  371.6 123.3 %all-to-all-start.2 = ((bf16[8,128,768]{2,1,0:T(8,128)(2,1)}), bf16[8,128,768]{2,1,0:T(8,128)(2,1)S(1)}, u32[]{:S(2)}, u32[]{:S(2)}) async-start(bf16[8,128,768]{2,1,0:T(8,128)(2,1)} %bitcast.40), calls=%async_computation.2 | async-start | bytes 3145728 | tf_op jit(solution)/shard_map/all_to_all | solution.py:335
  382.9 24.9 %collective-permute-start.54 = (bf16[2,2,2,48,768]{4,3,2,1,0:T(8,128)(2,1)S(1)}, bf16[2,2,2,48,768]{4,3,2,1,0:T(8,128)(2,1)S(1)}, u32[]{:S(2)}, u32[]{:S(2)}) collective-permute-start(bf16[2,2,2,48,768]{4,3,2,1,0:T(8,128)(2,1)S(1)} %dynamic-slice_bitcast_fusion.3), channel_id=1, source_target_pairs={{0,1},{1,0},{2,3},{3,2},{4,5},{5,4},{6,7},{7,6},{8,9},{9,8},{10,11... | collective-permute-start | bytes 1769480 | tf_op jit(solution)/shard_map/ppermute | solution.py:77
  387.6 33.2 %collective-permute-start.42 = (bf16[2,2,2,48,768]{4,3,2,1,0:T(8,128)(2,1)S(1)}, bf16[2,2,2,48,768]{4,3,2,1,0:T(8,128)(2,1)S(1)}, u32[]{:S(2)}, u32[]{:S(2)}) collective-permute-start(bf16[2,2,2,48,768]{4,3,2,1,0:T(8,128)(2,1)S(1)} %dynamic-slice_bitcast_fusion.5), channel_id=1, source_target_pairs={{0,1},{1,0},{2,3},{3,2},{4,5},{5,4},{6,7},{7,6},{8,9},{9,8},{10,11... | collective-permute-start | bytes 1769480 | tf_op jit(solution)/shard_map/ppermute | solution.py:77
  390.8 32.0 %collective-permute-start.37 = (bf16[2,2,2,48,768]{4,3,0,1,2:T(8,128)(2,1)S(1)}, bf16[2,2,2,48,768]{4,3,0,1,2:T(8,128)(2,1)S(1)}, u32[]{:S(2)}, u32[]{:S(2)}) collective-permute-start(bf16[2,2,2,48,768]{4,3,0,1,2:T(8,128)(2,1)S(1)} %dynamic-slice_bitcast_fusion.6), channel_id=1, source_target_pairs={{0,16},{8,24},{16,0},{24,8},{1,17},{9,25},{17,1},{25,9},{2,18},{10... | collective-permute-start | bytes 1769480 | tf_op jit(solution)/shard_map/ppermute | solution.py:77
  393.1 40.3 %collective-permute-start.30 = (bf16[2,2,2,48,768]{4,3,2,1,0:T(8,128)(2,1)S(1)}, bf16[2,2,2,48,768]{4,3,2,1,0:T(8,128)(2,1)S(1)}, u32[]{:S(2)}, u32[]{:S(2)}) collective-permute-start(bf16[2,2,2,48,768]{4,3,2,1,0:T(8,128)(2,1)S(1)} %dynamic-slice_bitcast_fusion.7), channel_id=1, source_target_pairs={{0,1},{1,0},{2,3},{3,2},{4,5},{5,4},{6,7},{7,6},{8,9},{9,8},{10,11... | collective-permute-start | bytes 1769480 | tf_op jit(solution)/shard_map/ppermute | solution.py:77
  407.8 40.0 %collective-permute-start.25 = (bf16[2,2,2,56,768]{4,3,2,1,0:T(8,128)(2,1)S(1)}, bf16[2,2,2,56,768]{4,3,2,1,0:T(8,128)(2,1)S(1)}, u32[]{:S(2)}, u32[]{:S(2)}) collective-permute-start(bf16[2,2,2,56,768]{4,3,2,1,0:T(8,128)(2,1)S(1)} %dynamic-slice_bitcast_fusion.2), channel_id=1, source_target_pairs={{0,16},{8,24},{16,0},{24,8},{1,17},{9,25},{17,1},{25,9},{2,18},{10... | collective-permute-start | bytes 2064392 | tf_op jit(solution)/shard_map/ppermute | solution.py:77
  409.0 26.5 %collective-permute-start.55 = (bf16[2,2,48,768]{3,2,1,0:T(8,128)(2,1)S(1)}, bf16[2,2,48,768]{3,2,1,0:T(8,128)(2,1)S(1)}, u32[]{:S(2)}, u32[]{:S(2)}) collective-permute-start(bf16[2,2,48,768]{3,2,1,0:T(8,128)(2,1)S(1)} %dynamic-slice_bitcast_fusion.9), channel_id=1, source_target_pairs={{0,16},{8,24},{16,0},{24,8},{1,17},{9,25},{17,1},{25,9},{2,18},{10... | collective-permute-start | bytes 884744 | tf_op jit(solution)/shard_map/ppermute | solution.py:77
  (112 other events, 1159.9 us)
